TPU v7x, 32 devices: a whole 2x2x4 slice. The times are simulated.
32 devices in a mesh: samp: 4 (over y, x), var: 8 (over z, core).
Axes of the slice: x: 2, y: 2, z: 4, core: 2. Of those that a mesh axis runs over, the one named last changes fastest.
Arguments:
- observed: bfloat16 [1024, 32768], P('samp', 'var'), may hold values from -6 to 6
- blocks: float32 [256, 2, 128, 128], P('var'), may hold values from -6 to 6
- diagonal: float32 [32768], P('var'), may hold values from 1 to 4
- pattern: int32 [256, 2], P('var'), may hold values from 0 to 255, as said below
Outputs:
- new_blocks: float32 [256, 2, 128, 128], P('var')
- new_diagonal: float32 [32768], P('var')
- objective: float32 [2], replicated
Inputs may be any that keep to these rules, and one draw needn't show every extreme that they name: pattern[c, 0] and pattern[c, 1] are two different row-block indices, one of them equal to c. For each index v of var, among its block columns c = v * 32 to v * 32 + 31, for every u, at most 4 of the entries that differ from c name row blocks in the range u * 32 to u * 32 + 31, and for some u exactly 4 do.
All inputs are finite; a program needn't handle non-finite values.
Results may differ from a plain program's by a relative error of at most 0.0049.
Values may be sent and summed in bfloat16 or wider, within the bound.
A program may use at most 128 MiB of HBM per device.

v0:
```python
import jax
import jax.numpy as jnp
from jax import lax
from jax.sharding import PartitionSpec as P

STEPS = 2


step_length = 0.5
penalty = 0.5


def shrink(moved, level):
    return jnp.sign(moved) * jnp.maximum(jnp.abs(moved) - level, 0.0)


def advance(diag_block, off_block, diag_values, grad_diag, grad_off, diag_mask, total_rows):
    grad_diag = grad_diag / total_rows
    grad_off = grad_off / total_rows
    new_off = shrink(off_block - step_length * grad_off, step_length * penalty)
    new_diag_block = jnp.where(
        diag_mask, 0.0, shrink(diag_block - step_length * grad_diag, step_length * penalty)
    )
    along = jnp.sum(jnp.where(diag_mask, grad_diag, 0.0), axis=1)
    moved = diag_values - step_length * along
    new_values = 0.5 * (moved + jnp.sqrt(moved * moved + 4.0 * step_length))
    return (new_diag_block, new_off, new_values)


def body(observed, blocks, diagonal, pattern):
    col_count = blocks.shape[0]
    block_width = blocks.shape[2]
    sample_rows = observed.shape[0]
    var_count = lax.axis_size("var")
    samp_count = lax.axis_size("samp")
    capacity = max(2, -(-col_count // var_count))
    total_rows = sample_rows * samp_count
    matrix_order = col_count * block_width * var_count
    var_index = lax.axis_index("var")
    column_ids = jnp.arange(col_count, dtype=jnp.int32)
    columns = var_index * col_count + column_ids
    on_diag = pattern == columns[:, None]
    off_row = jnp.sum(jnp.where(on_diag, 0, pattern), axis=1)
    owner_index = off_row // col_count
    resident_block = off_row % col_count
    earlier = (owner_index[None, :] == owner_index[:, None]) & (
        column_ids[None, :] < column_ids[:, None]
    )
    position_rank = jnp.sum(earlier, axis=1)
    slot_index = owner_index * capacity + position_rank
    all_slots = jnp.arange(var_count * capacity, dtype=jnp.int32)
    slot_match = slot_index[:, None] == all_slots[None, :]
    wanted = jnp.sum(jnp.where(slot_match, resident_block[:, None], 0), axis=0)
    asked_blocks = lax.all_to_all(wanted, "var", split_axis=0, concat_axis=0, tiled=True)
    nearby_panels = observed.reshape(sample_rows, col_count, block_width)
    outgoing = jnp.take(nearby_panels, asked_blocks, axis=1)
    arrived = lax.all_to_all(outgoing, "var", split_axis=1, concat_axis=1, tiled=True)
    distant_panels = jnp.take(arrived, slot_index, axis=1)
    diag_mask = jnp.eye(block_width, dtype=bool)
    flags = on_diag[:, :, None, None]
    diag_block = jnp.sum(jnp.where(flags, blocks, 0.0), axis=1)
    diag_block = jnp.where(diag_mask, 0.0, diag_block)
    off_block = jnp.sum(jnp.where(flags, 0.0, blocks), axis=1)
    diag_values = diagonal.reshape(col_count, block_width)
    samp_first = (lax.axis_index("samp") == 0).astype(jnp.float32)
    objective_parts = []
    for iteration in range(STEPS):
        full_diag = jnp.where(diag_mask, diag_values[:, None, :], diag_block)
        product = jnp.einsum(
            "qlh,lhy->qly",
            nearby_panels,
            full_diag.astype(jnp.bfloat16),
            preferred_element_type=jnp.float32,
        )
        product = product + jnp.einsum(
            "qlh,lhy->qly",
            distant_panels,
            off_block.astype(jnp.bfloat16),
            preferred_element_type=jnp.float32,
        )
        squares = jnp.sum(product * product)
        local_terms = -jnp.sum(jnp.log(diag_values)) + penalty * (
            jnp.sum(jnp.abs(diag_block)) + jnp.sum(jnp.abs(off_block))
        )
        part_value = (squares / (2.0 * total_rows) + samp_first * local_terms) / matrix_order
        objective_parts.append(part_value)
        lower_precision_product = product.astype(jnp.bfloat16)
        grad_diag = jnp.einsum(
            "rei,reo->eio",
            nearby_panels,
            lower_precision_product,
            preferred_element_type=jnp.float32,
        )
        grad_off = jnp.einsum(
            "rei,reo->eio",
            distant_panels,
            lower_precision_product,
            preferred_element_type=jnp.float32,
        )
        grad_diag, grad_off = lax.psum((grad_diag, grad_off), "samp")
        diag_block, off_block, diag_values = advance(
            diag_block, off_block, diag_values, grad_diag, grad_off, diag_mask, total_rows
        )
    objective = lax.psum(jnp.stack(objective_parts), ("samp", "var"))
    new_blocks = jnp.where(flags, diag_block[:, None], off_block[:, None])
    return (new_blocks, diag_values.reshape(-1), objective)


def solution(mesh):
    placed = (P("samp", "var"), P("var", None, None, None), P("var"), P("var", None))
    return jax.shard_map(
        body,
        mesh=mesh,
        in_specs=placed,
        out_specs=(P("var", None, None, None), P("var"), P()),
        check_vma=False,
    )
```

profile of v0, /device:TPU:0, one launch (start us, length us, event | category | flops | bytes accessed | tf_op | source)
XLA Modules:
  0.0 387.5 jit_solution(3992199303328004079)
XLA Ops:
  8.9 6.4 %all-to-all-start = ((s32[8,4,1]{1,2,0:T(1,128)}), s32[8,4,1]{1,2,0:T(1,128)S(1)}, u32[]{:S(2)}, u32[]{:S(2)}) async-start(s32[8,4,1]{1,2,0:T(1,128)} %bitcast.2), calls=%async_computation | async-start | bytes 8192 | tf_op jit(solution)/shard_map/all_to_all | solution.py:54
  15.2 3.3 copy.65
  18.5 2.9 copy.68
  22.6 3.8 gather_fusion
  26.4 3.2 select_bitcast_fusion
  29.6 5.2 %all-to-all-start.1 = ((bf16[256,32,128]{2,0,1:T(8,128)(2,1)}), bf16[256,32,128]{2,0,1:T(8,128)(2,1)}, u32[]{:S(2)}, u32[]{:S(2)}) async-start(bf16[256,32,128]{2,0,1:T(8,128)(2,1)} %select_bitcast_fusion), calls=%async_computation.1 | async-start | bytes 4194304 | tf_op jit(solution)/shard_map/all_to_all | solution.py:57
  35.0 5.9 %select_reduce_fusion = (f32[32,128,128]{2,1,0:T(8,128)}, f32[32,128,128]{2,1,0:T(8,128)}) fusion(f32[32,2,128,128]{3,2,1,0:T(8,128)} %param.7, pred[32,2]{1,0:T(8,128)(4,1)S(1)} %copy.63), kind=kLoop, calls=%fused_computation.4 | loop fusion | flops 3145728 | bytes 8388672 | tf_op jit(solution)/shard_map/reduce_sum | solution.py:63
  40.9 2.9 copy.64
  43.9 4.4 %fusion.18 = f32[32,128,256]{2,1,0:T(8,128)} fusion(bf16[256,32,128]{0,2,1:T(8,128)(2,1)S(1)} %bitcast.57, f32[32,128,128]{1,2,0:T(8,128)} %copy.64, f32[32,128]{1,0:T(8,128)S(1)} %bitcast.61, pred[128,128]{0,1:T(8,128)(4,1)S(1)} %iota_compare_fusion), kind=kOutput, calls=%fused_computation.37 | convolution fusion | flops 269484032 | bytes 8421376 | tf_op jit(solution)/shard_map/qlh,lhy->qly/dot_general | solution.py:69
  48.3 35.7 %all-to-all-done.1 = bf16[256,32,128]{2,0,1:T(8,128)(2,1)} async-done(((bf16[256,32,128]{2,0,1:T(8,128)(2,1)}), bf16[256,32,128]{2,0,1:T(8,128)(2,1)}, u32[]{:S(2)}, u32[]{:S(2)}) %all-to-all-start.1) | async-done | bytes 2097184 | tf_op jit(solution)/shard_map/all_to_all | solution.py:57
  84.0 3.7 gather_fusion.1
  87.7 5.6 %multiply_reduce_fusion.1 = (f32[]{:T(128)}, bf16[32,128,256]{2,1,0:T(8,128)(2,1)S(1)}) fusion(f32[32,128,256]{2,1,0:T(8,128)} %fusion.18, bf16[32,256,128]{2,1,0:T(8,128)(2,1)} %gather_fusion.1, pred[32]{0:T(512)(128)(4,1)S(1)} %get-tuple-element.16, f32[32,128,128]{2,1,0:T(8,128)} %get-tuple-element.4), kind=kOutput, calls=%fused_computation.3 | convolution fusion | flops 274202624 | bytes 10485796 | tf_op jit(solution)/shard_map/qlh,lhy->qly/dot_general | solution.py:75
  93.4 2.1 fusion.4
  97.8 2.9 copy.75
  100.7 99.6 %all-reduce.7.cloned.1.call-done = (f32[32,128,128]{1,2,0:T(8,128)}, f32[32,128,128]{1,2,0:T(8,128)}) async-done(((f32[32,128,128]{1,2,0:T(8,128)}, f32[32,128,128]{1,2,0:T(8,128)}), (f32[32,128,128]{1,2,0:T(8,128)}, f32[32,128,128]{1,2,0:T(8,128)})) %all-reduce.7.cloned.1.call-update) | async-done | bytes 4194320 | tf_op jit(solution)/shard_map/psum | solution.py:100
  200.3 4.7 %abs_reduce_fusion.3 = (f32[]{:T(128)}, f32[32,128]{1,0:T(8,128)S(1)}, f32[]{:T(128)}, f32[32,128,128]{1,2,0:T(8,128)S(1)}) fusion(f32[32,128,128]{1,2,0:T(8,128)} %copy.64, pred[128,128]{0,1:T(8,128)(4,1)S(1)} %iota_compare_fusion, f32[32,128,128]{1,2,0:T(8,128)} %get-tuple-element.12), kind=kLoop, calls=%fused_computation.24 | loop fusion | flops 8384510 | bytes 6324232 | tf_op jit(solution)/shard_map/reduce_sum | solution.py:83
  208.6 2.3 multiply_reduce_fusion
  210.9 2.1 fusion
  213.0 2.1 fusion.15
  220.6 98.3 %all-reduce.5.cloned.1.call-done = (f32[32,128,128]{1,2,0:T(8,128)}, f32[32,128,128]{1,2,0:T(8,128)}) async-done(((f32[32,128,128]{1,2,0:T(8,128)}, f32[32,128,128]{1,2,0:T(8,128)}), (f32[32,128,128]{1,2,0:T(8,128)}, f32[32,128,128]{1,2,0:T(8,128)})) %all-reduce.5.cloned.1.call-update) | async-done | bytes 4194320 | tf_op jit(solution)/shard_map/psum | solution.py:100
  318.9 9.0 %abs_reduce_fusion = (f32[]{:T(128)}, f32[32,128,128]{1,2,0:T(8,128)}, f32[32,128,128]{1,2,0:T(8,128)S(1)}, f32[32,128]{1,0:T(8,128)S(1)}) fusion(f32[32,128,128]{1,2,0:T(8,128)} %copy.75, f32[32,128,128]{1,2,0:T(8,128)} %get-tuple-element.13, f32[32,128,128]{1,2,0:T(8,128)} %get-tuple-element.10, f32[32,128,128]{1,2,0:T(8,128)} %copy-done.4, ...), kind=kLoop, calls=%fused_computation.21 | loop fusion | flops 14151679 | bytes 14712836 | tf_op jit(solution)/shard_map/reduce_sum | solution.py:83
  332.0 2.9 copy.81
  334.9 39.2 %psum.39 = f32[2]{0:T(128)} all-reduce(f32[2]{0:T(128)S(1)} %pad_maximum_fusion), channel_id=1, replica_groups=mesh['samp'=4,'var'=8] {'samp','var'}, use_global_device_ids=true, to_apply=%region_19.21 | all-reduce | flops 2 | bytes 16 | tf_op jit(solution)/shard_map/psum | solution.py:104
  375.9 4.7 %broadcast_select_fusion = f32[32,2,128,128]{3,2,1,0:T(8,128)} fusion(f32[32,128,128]{2,1,0:T(8,128)} %copy.81, f32[32,128,128]{2,1,0:T(8,128)} %copy.77, pred[32,2]{1,0:T(8,128)(4,1)S(1)} %copy.63), kind=kLoop, calls=%fused_computation.26 | loop fusion | flops 1048576 | bytes 8388672 | tf_op jit(solution)/shard_map/jit(_where)/select_n | solution.py:105
  (46 shorter events, 15.0 us)
Async XLA Ops:
  8.9 12.5 %all-to-all-start = ((s32[8,4,1]{1,2,0:T(1,128)}), s32[8,4,1]{1,2,0:T(1,128)S(1)}, u32[]{:S(2)}, u32[]{:S(2)}) async-start(s32[8,4,1]{1,2,0:T(1,128)} %bitcast.2), calls=%async_computation | async-start | bytes 8192 | tf_op jit(solution)/shard_map/all_to_all | solution.py:54
  29.6 5.3 %copy-start.7 = (s32[32,2]{0,1:T(2,128)S(1)}, s32[32,2]{0,1:T(2,128)}, u32[]{:S(2)}) copy-start(s32[32,2]{0,1:T(2,128)} %param.9) | copy-start | bytes 772
  29.6 54.4 %all-to-all-start.1 = ((bf16[256,32,128]{2,0,1:T(8,128)(2,1)}), bf16[256,32,128]{2,0,1:T(8,128)(2,1)}, u32[]{:S(2)}, u32[]{:S(2)}) async-start(bf16[256,32,128]{2,0,1:T(8,128)(2,1)} %select_bitcast_fusion), calls=%async_computation.1 | async-start | bytes 4194304 | tf_op jit(solution)/shard_map/all_to_all | solution.py:57
  34.8 165.4 %all-reduce.7.cloned.1.call-start = ((), (), s32[]{:S(2)}) async-start(), calls=%async_computation.3 | async-start | bytes 8388608 | tf_op jit(solution)/shard_map/psum | solution.py:100
  40.9 3.0 copy-start.6
  87.7 5.7 %copy-start = (bf16[32,256,128]{2,1,0:T(8,128)(2,1)S(1)}, bf16[32,256,128]{2,1,0:T(8,128)(2,1)}, u32[]{:S(2)}) copy-start(bf16[32,256,128]{2,1,0:T(8,128)(2,1)} %gather_fusion.1) | copy-start | bytes 6291460
  97.5 221.3 %all-reduce.5.cloned.1.call-start = ((), (), s32[]{:S(2)}) async-start(), calls=%async_computation.2 | async-start | bytes 8388608 | tf_op jit(solution)/shard_map/psum | solution.py:100
  204.9 1.3 copy-start.4
  205.0 2.3 copy-start.1
  205.0 3.0 copy-start.3
  205.0 3.6 copy-start.5
  215.1 1.6 copy-start.2
Sparse Core Ops, SparseCore 0:
  97.7 102.5 all-reduce.6
  215.2 103.5 all-reduce.4
where the time goes:
time: 388 us; the launch traced here: 387 us
  waiting for transfers between devices  234 us (60%)
  blocking collectives  39.2 us (10%)
  other arithmetic  31.9 us (8%)
  local copies, waits for them, and re-layouts  29.6 us (8%)
  matrix products  21.8 us (6%)
  between operations  19.5 us (5%)
  starting transfers between devices  11.8 us (3%)
    psum x2, waiting for transfers between devices, body(): grad_diag, grad_off = lax.psum((grad_diag, grad_off), 'samp')  198 us
    psum x1, blocking collectives, body(): objective = lax.psum(jnp.stack(objective_parts), ('samp', 'var'))  39.2 us
    all_to_all x1, waiting for transfers between devices, body(): lax.all_to_all(outgoing, 'var', split_axis=1, concat_axis=1, tiled=True)  35.7 us
    reduce_sum x2, other arithmetic, body(): jnp.sum(jnp.abs(off_block))  10.3 us
    dot_general x2, matrix products, body(): jnp.einsum('qlh,lhy->qly', distant_panels, off_block.astype(jnp.bfloat16)...  7.97 us
  transfers between devices with their start and end apart: 4, of which 3 were waited for; matrix products, arithmetic and copies ran while one was open for 6% of the time, Pallas kernels for 0%

commit v1 on v0

--- a/solution.py
+++ b/solution.py
@@ -1,6 +1,10 @@
+import functools
+
 import jax
 import jax.numpy as jnp
 from jax import lax
+from jax.experimental import pallas as pl
+from jax.experimental.pallas import tpu as pltpu
 from jax.sharding import PartitionSpec as P
 
 STEPS = 2
@@ -8,10 +12,301 @@
 
 step_length = 0.5
 penalty = 0.5
+MESH = pl.DeviceIdType.MESH
 
 
 def shrink(moved, level):
-    return jnp.sign(moved) * jnp.maximum(jnp.abs(moved) - level, 0.0)
+    return moved - jnp.clip(moved, -level, level)
+
+
+def flip(index, offset, count):
+    out, bit = 0, 1
+    while bit < count:
+        out = out + ((index // bit + offset // bit) % 2) * bit
+        bit *= 2
+    return out
+
+
+def pack_kernel(samp, var, near_idx, far_idx, own_slot, x_ref, blk_hbm, dia_ref,
+                near_ref, far_ref, own_ref, odia_ref, sem):
+    width = dia_ref.shape[1]
+    me = lax.axis_index("samp")
+    copies = []
+    for u in range(var):
+        col = near_idx[u * samp + me]
+        slot = own_slot[u * samp + me]
+        for part in range(2):
+            which = slot if part == 0 else 1 - slot
+            copy = pltpu.make_async_copy(blk_hbm.at[col, which], own_ref.at[u, part], sem.at[u, part])
+            copy.start()
+            copies.append(copy)
+        odia_ref[pl.ds(u, 1), :] = dia_ref[pl.ds(col, 1), :]
+    for u in range(var):
+        for k in range(samp):
+            at = u * samp + k
+            near = pl.multiple_of(near_idx[at] * width, width)
+            near_ref[k, u] = x_ref[:, pl.ds(near, width)]
+            far = pl.multiple_of(far_idx[at] * width, width)
+            far_ref[u, k] = x_ref[:, pl.ds(far, width)]
+    for copy in copies:
+        copy.wait()
+
+
+def main_kernel(samp, var, near_ref, far_ref, blk_ref, dia_ref, fin_ref, tails_ref, obj_ref,
+                nearbuf, farz, farbuf, oz, acc,
+                near_s, near_r, z_s, z_r, fwd_s, fwd_r, out_s, out_r,
+                nloc, floc, zloc, tail_s, tail_r, oz_s, oz_r):
+    s = lax.axis_index("samp")
+    v = lax.axis_index("var")
+    rows, width = near_ref.shape[2], near_ref.shape[3]
+    total_rows = rows * samp
+
+    barrier = pltpu.get_barrier_semaphore()
+    for d in range(1, samp):
+        pl.semaphore_signal(barrier, inc=1, device_id={"samp": flip(s, d, samp)}, device_id_type=MESH)
+    for i in range(1, var):
+        pl.semaphore_signal(barrier, inc=1, device_id={"var": flip(v, i, var)}, device_id_type=MESH)
+    pl.semaphore_wait(barrier, samp + var - 2)
+
+    def z_copy(i):
+        u = flip(v, i, var)
+        return pltpu.make_async_remote_copy(
+            src_ref=far_ref.at[u], dst_ref=farz.at[v], send_sem=z_s.at[i], recv_sem=z_r.at[i],
+            device_id={"var": u}, device_id_type=MESH)
+
+    def near_copy(d, i):
+        u, k = flip(v, i, var), flip(s, d, samp)
+        return pltpu.make_async_remote_copy(
+            src_ref=near_ref.at[k, u], dst_ref=nearbuf.at[s, u],
+            send_sem=near_s.at[d, i], recv_sem=near_r.at[d, i],
+            device_id={"samp": k}, device_id_type=MESH)
+
+    def fwd_copy(d, i):
+        u, k = flip(v, i, var), flip(s, d, samp)
+        return pltpu.make_async_remote_copy(
+            src_ref=farz.at[u, k], dst_ref=farbuf.at[u, s],
+            send_sem=fwd_s.at[d, i], recv_sem=fwd_r.at[d, i],
+            device_id={"samp": k}, device_id_type=MESH)
+
+    def out_copy(d, i):
+        u, k = flip(v, i, var), flip(s, d, samp)
+        return pltpu.make_async_remote_copy(
+            src_ref=fin_ref.at[s, u], dst_ref=fin_ref.at[s, u],
+            send_sem=out_s.at[d, i], recv_sem=out_r.at[d, i],
+            device_id={"samp": k}, device_id_type=MESH)
+
+    def near_local(i):
+        u = flip(v, i, var)
+        return pltpu.make_async_copy(near_ref.at[s, u], nearbuf.at[s, u], nloc.at[i])
+
+    def far_local(i):
+        u = flip(v, i, var)
+        return pltpu.make_async_copy(farz.at[u, s], farbuf.at[u, s], floc.at[i])
+
+    def z_local():
+        return pltpu.make_async_copy(far_ref.at[v], farz.at[v], zloc)
+
+    def forward(i):
+        for d in range(1, samp):
+            fwd_copy(d, i).start()
+        far_local(i).start()
+
+    def start_near(i):
+        for d in range(1, samp):
+            near_copy(d, i).start()
+        near_local(i).start()
+
+    eye = lax.broadcasted_iota(jnp.int32, (width, width), 0) == lax.broadcasted_iota(
+        jnp.int32, (width, width), 1)
+
+    def column(i):
+        u = flip(v, i, var)
+        for d in range(1, samp):
+            near_copy(d, i).wait_recv()
+            fwd_copy(d, i).wait_recv()
+        near_local(i).wait()
+        far_local(i).wait()
+        a = jnp.concatenate([nearbuf[p, u] for p in range(samp)], axis=0)
+        b = jnp.concatenate([farbuf[u, p] for p in range(samp)], axis=0)
+        wd = jnp.where(eye, 0.0, blk_ref[u, 0])
+        wo = blk_ref[u, 1]
+        dv = dia_ref[pl.ds(u, 1), :]
+        over_first = (((0,), (0,)), ((), ()))
+        for step in range(STEPS):
+            rd = jnp.where(eye, dv, wd).astype(jnp.bfloat16)
+            ro = wo.astype(jnp.bfloat16)
+            product = jnp.dot(a, rd, preferred_element_type=jnp.float32)
+            product = product + jnp.dot(b, ro, preferred_element_type=jnp.float32)
+            terms = (jnp.sum(product * product, axis=0, keepdims=True) / (2.0 * total_rows)
+                     - jnp.log(dv)
+                     + penalty * jnp.sum(jnp.abs(wd) + jnp.abs(wo), axis=0, keepdims=True))
+            acc[step:step + 1, :] += terms
+            low = product.astype(jnp.bfloat16)
+            gd = lax.dot_general(a, low, over_first, preferred_element_type=jnp.float32) / total_rows
+            go = lax.dot_general(b, low, over_first, preferred_element_type=jnp.float32) / total_rows
+            wo = shrink(wo - step_length * go, step_length * penalty)
+            wd = jnp.where(eye, 0.0, shrink(wd - step_length * gd, step_length * penalty))
+            along = jnp.sum(jnp.where(eye, gd, 0.0), axis=0, keepdims=True)
+            moved = dv - step_length * along
+            dv = 0.5 * (moved + jnp.sqrt(moved * moved + 4.0 * step_length))
+        fin_ref[s, u, 0] = wd.astype(jnp.bfloat16)
+        fin_ref[s, u, 1] = wo.astype(jnp.bfloat16)
+        tails_ref[s, pl.ds(u, 1), :] = dv
+        for d in range(1, samp):
+            out_copy(d, i).start()
+
+    acc[...] = jnp.zeros_like(acc)
+    z_local().start()
+    lax.fori_loop(1, var, lambda i, c: (z_copy(i).start(), c)[1], 0)
+    start_near(0)
+    z_local().wait()
+    forward(0)
+    lax.fori_loop(1, var, lambda i, c: (start_near(i), c)[1], 0)
+
+    def turn(i, carry):
+        @pl.when(i < var)
+        def _():
+            z_copy(i).wait_recv()
+            forward(i)
+
+        column(i - 1)
+        return carry
+
+    lax.fori_loop(1, var + 1, turn, 0)
+
+    tails_ref[s, var:, :] = acc[...]
+
+    def tail_copy(d):
+        return pltpu.make_async_remote_copy(
+            src_ref=tails_ref.at[s], dst_ref=tails_ref.at[s],
+            send_sem=tail_s.at[d], recv_sem=tail_r.at[d],
+            device_id={"samp": flip(s, d, samp)}, device_id_type=MESH)
+
+    def oz_copy(i):
+        return pltpu.make_async_remote_copy(
+            src_ref=oz.at[v], dst_ref=oz.at[v], send_sem=oz_s.at[i], recv_sem=oz_r.at[i],
+            device_id={"var": flip(v, i, var)}, device_id_type=MESH)
+
+    for d in range(1, samp):
+        tail_copy(d).start()
+    for d in range(1, samp):
+        tail_copy(d).wait_recv()
+    group = tails_ref[0, var:, :]
+    for k in range(1, samp):
+        group = group + tails_ref[k, var:, :]
+    oz[v] = group
+    for i in range(1, var):
+        oz_copy(i).start()
+    for i in range(1, var):
+        oz_copy(i).wait_recv()
+    whole = oz[0]
+    for u in range(1, var):
+        whole = whole + oz[u]
+    obj_ref[...] = whole
+
+    def finish(i, carry):
+        for d in range(1, samp):
+            near_copy(d, i).wait_send()
+            fwd_copy(d, i).wait_send()
+            out_copy(d, i).wait()
+        return carry
+
+    lax.fori_loop(0, var, finish, 0)
+    for d in range(1, samp):
+        tail_copy(d).wait_send()
+    for i in range(1, var):
+        z_copy(i).wait_send()
+        oz_copy(i).wait_send()
+
+
+def unpack_kernel(group, owner, rank, slot, fin_ref, tails_ref, out_ref, dia_ref):
+    first = pl.program_id(0) * group
+    for j in range(group):
+        col = first + j
+        k, u, at = rank[col], owner[col], slot[col]
+        out_ref[j, 0] = fin_ref[k, u, at].astype(jnp.float32)
+        out_ref[j, 1] = fin_ref[k, u, 1 - at].astype(jnp.float32)
+        dia_ref[pl.ds(col, 1), :] = tails_ref[k, pl.ds(u, 1), :]
+
+
+def column_body(observed, blocks, diagonal, pattern):
+    cols, width = blocks.shape[0], blocks.shape[2]
+    rows = observed.shape[0]
+    var, samp = lax.axis_size("var"), lax.axis_size("samp")
+    v = lax.axis_index("var")
+    ids = jnp.arange(cols, dtype=jnp.int32)
+    on_diag = pattern == (v * cols + ids)[:, None]
+    off_row = jnp.sum(jnp.where(on_diag, 0, pattern), axis=1)
+    diag_slot = jnp.where(on_diag[:, 1], 1, 0).astype(jnp.int32)
+    owner = off_row // cols
+    resident = off_row % cols
+    earlier = (owner[None, :] == owner[:, None]) & (ids[None, :] < ids[:, None])
+    rank = jnp.sum(earlier, axis=1).astype(jnp.int32)
+    slot_index = owner * samp + rank
+    match = slot_index[:, None] == ids[None, :]
+    wanted = jnp.sum(jnp.where(match, resident[:, None], 0), axis=0)
+    near_idx = jnp.sum(jnp.where(match, ids[:, None], 0), axis=0)
+    own_slot = jnp.sum(jnp.where(match, diag_slot[:, None], 0), axis=0)
+    asked = lax.all_to_all(wanted, "var", split_axis=0, concat_axis=0, tiled=True)
+
+    vmem = pl.BlockSpec(memory_space=pltpu.VMEM)
+    smem = pl.BlockSpec(memory_space=pltpu.SMEM)
+    hbm = pl.BlockSpec(memory_space=pl.ANY)
+    near, far, own, own_dia = pl.pallas_call(
+        functools.partial(pack_kernel, samp, var),
+        out_shape=(
+            jax.ShapeDtypeStruct((samp, var, rows, width), observed.dtype),
+            jax.ShapeDtypeStruct((var, samp, rows, width), observed.dtype),
+            jax.ShapeDtypeStruct((var, 2, width, width), jnp.float32),
+            jax.ShapeDtypeStruct((var, width), jnp.float32),
+        ),
+        in_specs=[smem, smem, smem, vmem, hbm, vmem],
+        out_specs=(vmem,) * 4,
+        scratch_shapes=[pltpu.SemaphoreType.DMA((var, 2))],
+        name="pack",
+    )(near_idx, asked, own_slot, observed, blocks, diagonal.reshape(cols, width))
+
+    dma = pltpu.SemaphoreType.DMA
+    fin, tails, whole = pl.pallas_call(
+        functools.partial(main_kernel, samp, var),
+        out_shape=(
+            jax.ShapeDtypeStruct((samp, var, 2, width, width), jnp.bfloat16),
+            jax.ShapeDtypeStruct((samp, var + 8, width), jnp.float32),
+            jax.ShapeDtypeStruct((8, width), jnp.float32),
+        ),
+        in_specs=[vmem] * 4,
+        out_specs=(vmem,) * 3,
+        scratch_shapes=[
+            pltpu.VMEM((samp, var, rows, width), observed.dtype),
+            pltpu.VMEM((var, samp, rows, width), observed.dtype),
+            pltpu.VMEM((var, samp, rows, width), observed.dtype),
+            pltpu.VMEM((var, 8, width), jnp.float32),
+            pltpu.VMEM((8, width), jnp.float32),
+            dma((samp, var)), dma((samp, var)), dma((var,)), dma((var,)),
+            dma((samp, var)), dma((samp, var)), dma((samp, var)), dma((samp, var)),
+            dma((var,)), dma((var,)), dma, dma((samp,)), dma((samp,)), dma((var,)), dma((var,)),
+        ],
+        compiler_params=pltpu.CompilerParams(collective_id=0, has_side_effects=True),
+        name="columns",
+    )(near, far, own, own_dia)
+
+    group = 4
+    new_blocks, new_diagonal = pl.pallas_call(
+        functools.partial(unpack_kernel, group),
+        out_shape=(
+            jax.ShapeDtypeStruct(blocks.shape, jnp.float32),
+            jax.ShapeDtypeStruct((cols, width), jnp.float32),
+        ),
+        grid=(cols // group,),
+        in_specs=[smem, smem, smem, vmem, vmem],
+        out_specs=(
+            pl.BlockSpec((group, 2, width, width), lambda g: (g, 0, 0, 0)),
+            pl.BlockSpec((cols, width), lambda g: (0, 0)),
+        ),
+        name="unpack",
+    )(owner, rank, diag_slot, fin, tails)
+    objective = jnp.sum(whole[:STEPS], axis=1) / (cols * width * var)
+    return new_blocks, new_diagonal.reshape(-1), objective
 
 
 def advance(diag_block, off_block, diag_values, grad_diag, grad_off, diag_mask, total_rows):
@@ -106,10 +401,23 @@
     return (new_blocks, diag_values.reshape(-1), objective)
 
 
+def power_of_two(count):
+    return count & (count - 1) == 0
+
+
+def whole_body(observed, blocks, diagonal, pattern):
+    cols = blocks.shape[0]
+    var, samp = lax.axis_size("var"), lax.axis_size("samp")
+    exact = samp * var == cols and cols % 4 == 0 and var % 8 == 0 and blocks.shape[2] == 128
+    if exact and power_of_two(samp) and power_of_two(var):
+        return column_body(observed, blocks, diagonal, pattern)
+    return body(observed, blocks, diagonal, pattern)
+
+
 def solution(mesh):
     placed = (P("samp", "var"), P("var", None, None, None), P("var"), P("var", None))
     return jax.shard_map(
-        body,
+        whole_body,
         mesh=mesh,
         in_specs=placed,
         out_specs=(P("var", None, None, None), P("var"), P()),

time: 388 us -> 112 us (0.29)
  waiting for transfers between devices: 234 us -> 0 us
  Pallas kernels: 0 us -> 93.8 us
  local copies, waits for them, and re-layouts: 29.6 us -> 1.26 us
  other arithmetic: 31.9 us -> 4.19 us
  blocking collectives: 39.2 us -> 11.7 us
  matrix products: 21.8 us -> 0 us
  between operations: 19.5 us -> 0.72 us
  starting transfers between devices: 11.8 us -> 0 us
    psum x2 -> x0, waiting for transfers between devices: 198 us -> none  [body(): grad_diag, grad_off = lax.psum((grad_diag, grad_off), 'samp')]
    pallas_call x0 -> x3, Pallas kernels: none -> 93.8 us  [the longest x1 83.3 us: column_body(): pl.pallas_call(functools.partial(main_kernel, samp, var), out_shape=(jax....]
    psum x1 -> x0, blocking collectives: 39.2 us -> none  [body(): objective = lax.psum(jnp.stack(objective_parts), ('samp', 'var'))]
    all_to_all x2 -> x0, waiting for transfers between devices: 35.7 us -> none  [the longest x1 35.7 us: body(): lax.all_to_all(outgoing, 'var', split_axis=1, concat_axis=1, tiled=True)]
    dot_general x8 -> x0, matrix products: 21.8 us -> none  [the longest x2 7.97 us: body(): jnp.einsum('qlh,lhy->qly', distant_panels, off_block.astype(jnp.bfloat16)...]
    reduce_sum x8 -> x4, other arithmetic: 23.2 us -> 2.3 us  [the longest x1 0.79 us: column_body(): objective = jnp.sum(whole[:STEPS], axis=1) / (cols * width * var)]
    all_to_all x0 -> x1, blocking collectives: none -> 11.7 us  [column_body(): lax.all_to_all(wanted, 'var', split_axis=0, concat_axis=0, tiled=True)]
    all_to_all x2 -> x0, starting transfers between devices: 11.6 us -> none  [the longest x1 6.35 us: body(): lax.all_to_all(wanted, 'var', split_axis=0, concat_axis=0, tiled=True)]
  transfers between devices with their start and end apart: 4 -> 0, of which waited for: 3 -> 0; matrix products, arithmetic and copies ran while one was open for 6% -> 0% of each run, Pallas kernels for 0% -> 0%
where the time goes in v1:
time: 112 us
  Pallas kernels  93.8 us (84%)
  blocking collectives  11.7 us (10%)
  other arithmetic  4.19 us (4%)
  local copies, waits for them, and re-layouts  1.26 us (1%)
    pallas_call x1, Pallas kernels, column_body(): pl.pallas_call(functools.partial(main_kernel, samp, var), out_shape=(jax....  83.3 us
    all_to_all x1, blocking collectives, column_body(): lax.all_to_all(wanted, 'var', split_axis=0, concat_axis=0, tiled=True)  11.7 us
    pallas_call x1, Pallas kernels, column_body(): pl.pallas_call(functools.partial(pack_kernel, samp, var), out_shape=(jax....  5.35 us
    pallas_call x1, Pallas kernels, column_body(): pl.pallas_call(functools.partial(unpack_kernel, group), out_shape=(jax.Sh...  5.15 us

profile of v1, /device:TPU:0, one launch (start us, length us, event | category | flops | bytes accessed | tf_op | source)
XLA Modules:
  0.0 111.7 jit_solution(9681013229908402576)
XLA Ops:
  0.6 0.7 select_reduce_fusion.3
  1.3 0.7 broadcast_compare_fusion
  2.0 0.0 copy-start
  2.1 0.0 copy-start.1
  2.1 0.2 convert_reduce_fusion.rank
  2.3 0.0 copy-start.2
  2.3 0.6 select_reduce_fusion
  2.9 0.1 all_to_all.7
  3.0 11.7 %all_to_all.11 = s32[8,4,1]{1,2,0:T(1,128)S(1)} all-to-all(s32[8,4,1]{1,2,0:T(1,128)S(1)} %bitcast.7), channel_id=1, replica_groups=mesh['samp'=4,'var'=8] {'var'}, dimensions={0} | all-to-all | bytes 256 | tf_op jit(solution)/shard_map/all_to_all | solution.py:250
  14.7 0.5 broadcast.143
  15.2 0.7 reduce.3
  15.9 0.7 all_to_all.9.far_idx
  16.6 5.4 %pack.1 = (bf16[4,8,256,128]{3,2,1,0:T(8,128)(2,1)}, bf16[8,4,256,128]{3,2,1,0:T(8,128)(2,1)}, f32[8,2,128,128]{3,2,1,0:T(8,128)}, f32[8,128]{1,0:T(8,128)}) custom-call(s32[32]{0:T(128)} %get-tuple-element.23.near_idx, s32[32]{0:T(128)} %all_to_all.9.far_idx, s32[32]{0:T(128)} %get-tuple-element.21.own_slot, bf16[256,4096]{1,0:T(8,128)(2,1)} %x_ref.1, ...), custom_call_target="tpu_custom_call" | custom-call | tf_op jit(solution)/shard_map/pack/pallas_call | solution.py:255
  21.9 0.0 copy-done
  21.9 0.0 copy-done.1
  21.9 0.0 copy-done.2
  21.9 83.3 %columns.1 = (bf16[4,8,2,128,128]{4,3,2,1,0:T(8,128)(2,1)}, f32[4,16,128]{2,1,0:T(8,128)}, f32[8,128]{1,0:T(8,128)}) custom-call(bf16[4,8,256,128]{3,2,1,0:T(8,128)(2,1)} %get-tuple-element.12.near_ref, bf16[8,4,256,128]{3,2,1,0:T(8,128)(2,1)} %get-tuple-element.13.far_ref, f32[8,2,128,128]{3,2,1,0:T(8,128)} %get-tuple-element.14.blk_ref, ...), custom_call_target="tpu_custom_call" | custom-call | tf_op jit(solution)/shard_map/columns/pallas_call | solution.py:270
  105.2 0.8 slice_reduce_fusion
  106.0 0.5 broadcast_multiply_fusion
  106.5 5.1 %unpack.1 = (f32[32,2,128,128]{3,2,1,0:T(8,128)}, f32[32,128]{1,0:T(8,128)}) custom-call(s32[32]{0:T(128)} %copy-done.1, s32[32]{0:T(128)} %copy-done.2, s32[32]{0:T(128)} %copy-done, bf16[4,8,2,128,128]{4,3,2,1,0:T(8,128)(2,1)} %get-tuple-element.16.fin_ref, f32[4,16,128]{2,1,0:T(8,128)} %get-tuple-element.17.tails_ref), custom_call_target="tpu_custom_call" | custom-call | tf_op jit(solution)/shard_map/unpack/pallas_call | solution.py:294
  (4 shorter events, 0.0 us)
Async XLA Ops:
  2.0 19.9 %copy-start = (s32[32]{0:T(128)}, s32[32]{0:T(128)S(1)}, u32[]{:S(2)}) copy-start(s32[32]{0:T(128)S(1)} %fusion.1.slot) | copy-start | bytes 388
  2.1 19.9 %copy-start.1 = (s32[32]{0:T(128)}, s32[32]{0:T(128)S(1)}, u32[]{:S(2)}) copy-start(s32[32]{0:T(128)S(1)} %get-tuple-element.25.owner) | copy-start | bytes 388
  2.3 19.7 %copy-start.2 = (s32[32]{0:T(128)}, s32[32]{0:T(128)S(1)}, u32[]{:S(2)}) copy-start(s32[32]{0:T(128)S(1)} %convert_reduce_fusion.rank) | copy-start | bytes 388

commit v2 on v1

--- a/solution.py
+++ b/solution.py
@@ -25,6 +25,27 @@
         out = out + ((index // bit + offset // bit) % 2) * bit
         bit *= 2
     return out
+
+
+def ask_kernel(var, want_ref, asked_ref, got, send, recv):
+    v = lax.axis_index("var")
+    barrier = pltpu.get_barrier_semaphore()
+    for i in range(1, var):
+        pl.semaphore_signal(barrier, inc=1, device_id={"var": flip(v, i, var)}, device_id_type=MESH)
+    pl.semaphore_wait(barrier, var - 1)
+
+    def copy(i):
+        u = flip(v, i, var)
+        return pltpu.make_async_remote_copy(
+            src_ref=want_ref.at[u], dst_ref=got.at[v], send_sem=send.at[i], recv_sem=recv.at[i],
+            device_id={"var": u}, device_id_type=MESH)
+
+    for i in range(1, var):
+        copy(i).start()
+    got[v] = want_ref[v]
+    for i in range(1, var):
+        copy(i).wait()
+    asked_ref[...] = got[...]
 
 
 def pack_kernel(samp, var, near_idx, far_idx, own_slot, x_ref, blk_hbm, dia_ref,
@@ -46,75 +67,75 @@
             at = u * samp + k
             near = pl.multiple_of(near_idx[at] * width, width)
             near_ref[k, u] = x_ref[:, pl.ds(near, width)]
-            far = pl.multiple_of(far_idx[at] * width, width)
+            far = pl.multiple_of(far_idx[u, 0, k] * width, width)
             far_ref[u, k] = x_ref[:, pl.ds(far, width)]
     for copy in copies:
         copy.wait()
 
 
-def main_kernel(samp, var, near_ref, far_ref, blk_ref, dia_ref, fin_ref, tails_ref, obj_ref,
-                nearbuf, farz, farbuf, oz, acc,
-                near_s, near_r, z_s, z_r, fwd_s, fwd_r, out_s, out_r,
-                nloc, floc, zloc, tail_s, tail_r, oz_s, oz_r):
+def main_kernel(samp, var, near_ref, far_ref, blk_ref, dia_ref, fin_ref, tails_ref, obj_ref, farz, cc_out, cc_in, cc_own, oo_out, oo_in, oo_own, oz, acc,
+                cc_s, cc_r, z_s, z_r, oo_s, oo_r, out_s, out_r,
+                tail_s, tail_r, oz_s, oz_r):
     s = lax.axis_index("samp")
     v = lax.axis_index("var")
-    rows, width = near_ref.shape[2], near_ref.shape[3]
+    rows, width = farz.shape[2], farz.shape[3]
     total_rows = rows * samp
+    over_first = (((0,), (0,)), ((), ()))
 
     barrier = pltpu.get_barrier_semaphore()
+    for i in range(1, var):
+        pl.semaphore_signal(barrier, inc=1, device_id={"var": flip(v, i, var)}, device_id_type=MESH)
     for d in range(1, samp):
         pl.semaphore_signal(barrier, inc=1, device_id={"samp": flip(s, d, samp)}, device_id_type=MESH)
-    for i in range(1, var):
-        pl.semaphore_signal(barrier, inc=1, device_id={"var": flip(v, i, var)}, device_id_type=MESH)
     pl.semaphore_wait(barrier, samp + var - 2)
+
+    def remote(src, dst, send, recv, **where):
+        return pltpu.make_async_remote_copy(
+            src_ref=src, dst_ref=dst, send_sem=send, recv_sem=recv,
+            device_id=where, device_id_type=MESH)
 
     def z_copy(i):
         u = flip(v, i, var)
-        return pltpu.make_async_remote_copy(
-            src_ref=far_ref.at[u], dst_ref=farz.at[v], send_sem=z_s.at[i], recv_sem=z_r.at[i],
-            device_id={"var": u}, device_id_type=MESH)
-
-    def near_copy(d, i):
+        return remote(far_ref.at[u], farz.at[v], z_s.at[i], z_r.at[i], var=u)
+
+    def cc_copy(d, i):
         u, k = flip(v, i, var), flip(s, d, samp)
-        return pltpu.make_async_remote_copy(
-            src_ref=near_ref.at[k, u], dst_ref=nearbuf.at[s, u],
-            send_sem=near_s.at[d, i], recv_sem=near_r.at[d, i],
-            device_id={"samp": k}, device_id_type=MESH)
-
-    def fwd_copy(d, i):
+        return remote(cc_out.at[u, k], cc_in.at[u, s], cc_s.at[d, i], cc_r.at[d, i], samp=k)
+
+    def oo_copy(d, i):
         u, k = flip(v, i, var), flip(s, d, samp)
-        return pltpu.make_async_remote_copy(
-            src_ref=farz.at[u, k], dst_ref=farbuf.at[u, s],
-            send_sem=fwd_s.at[d, i], recv_sem=fwd_r.at[d, i],
-            device_id={"samp": k}, device_id_type=MESH)
+        return remote(oo_out.at[u, k], oo_in.at[u, s], oo_s.at[d, i], oo_r.at[d, i], samp=k)
 
     def out_copy(d, i):
         u, k = flip(v, i, var), flip(s, d, samp)
-        return pltpu.make_async_remote_copy(
-            src_ref=fin_ref.at[s, u], dst_ref=fin_ref.at[s, u],
-            send_sem=out_s.at[d, i], recv_sem=out_r.at[d, i],
-            device_id={"samp": k}, device_id_type=MESH)
-
-    def near_local(i):
+        return remote(fin_ref.at[s, u], fin_ref.at[s, u], out_s.at[d, i], out_r.at[d, i], samp=k)
+
+    def gram(left, right):
+        return lax.dot_general(left, right, over_first, preferred_element_type=jnp.float32)
+
+    def start_cc(i):
         u = flip(v, i, var)
-        return pltpu.make_async_copy(near_ref.at[s, u], nearbuf.at[s, u], nloc.at[i])
-
-    def far_local(i):
+        for d in range(samp):
+            k = flip(s, d, samp)
+            c = near_ref[k, u]
+            part = gram(c, c)
+            if d == 0:
+                cc_own[u] = part
+            else:
+                cc_out[u, k] = part.astype(jnp.bfloat16)
+                cc_copy(d, i).start()
+
+    def start_oo(i, far_panel):
         u = flip(v, i, var)
-        return pltpu.make_async_copy(farz.at[u, s], farbuf.at[u, s], floc.at[i])
-
-    def z_local():
-        return pltpu.make_async_copy(far_ref.at[v], farz.at[v], zloc)
-
-    def forward(i):
-        for d in range(1, samp):
-            fwd_copy(d, i).start()
-        far_local(i).start()
-
-    def start_near(i):
-        for d in range(1, samp):
-            near_copy(d, i).start()
-        near_local(i).start()
+        for d in range(samp):
+            k = flip(s, d, samp)
+            o = far_panel(u, k)
+            part = gram(o, jnp.concatenate([near_ref[k, u], o], axis=1))
+            if d == 0:
+                oo_own[u] = part
+            else:
+                oo_out[u, k] = part.astype(jnp.bfloat16)
+                oo_copy(d, i).start()
 
     eye = lax.broadcasted_iota(jnp.int32, (width, width), 0) == lax.broadcasted_iota(
         jnp.int32, (width, width), 1)
@@ -122,28 +143,32 @@
     def column(i):
         u = flip(v, i, var)
         for d in range(1, samp):
-            near_copy(d, i).wait_recv()
-            fwd_copy(d, i).wait_recv()
-        near_local(i).wait()
-        far_local(i).wait()
-        a = jnp.concatenate([nearbuf[p, u] for p in range(samp)], axis=0)
-        b = jnp.concatenate([farbuf[u, p] for p in range(samp)], axis=0)
+            cc_copy(d, i).wait_recv()
+            oo_copy(d, i).wait_recv()
+        cc, oo = cc_own[u], oo_own[u]
+        for d in range(1, samp):
+            p = flip(s, d, samp)
+            cc = cc + cc_in[u, p].astype(jnp.float32)
+            oo = oo + oo_in[u, p].astype(jnp.float32)
+        both = jnp.concatenate(
+            [jnp.concatenate([cc, oo[:, :width].T], axis=1), oo], axis=0)
+        high = both.astype(jnp.bfloat16)
+        low = (both - high.astype(jnp.float32)).astype(jnp.bfloat16)
+        gram_parts = jnp.concatenate([high, low], axis=1)
         wd = jnp.where(eye, 0.0, blk_ref[u, 0])
         wo = blk_ref[u, 1]
         dv = dia_ref[pl.ds(u, 1), :]
-        over_first = (((0,), (0,)), ((), ()))
         for step in range(STEPS):
-            rd = jnp.where(eye, dv, wd).astype(jnp.bfloat16)
-            ro = wo.astype(jnp.bfloat16)
-            product = jnp.dot(a, rd, preferred_element_type=jnp.float32)
-            product = product + jnp.dot(b, ro, preferred_element_type=jnp.float32)
-            terms = (jnp.sum(product * product, axis=0, keepdims=True) / (2.0 * total_rows)
-                     - jnp.log(dv)
+            rounded = jnp.concatenate(
+                [jnp.where(eye, dv, wd).astype(jnp.bfloat16), wo.astype(jnp.bfloat16)], axis=0)
+            grad = jnp.dot(gram_parts, jnp.concatenate([rounded, rounded], axis=0),
+                           preferred_element_type=jnp.float32)
+            squares = jnp.sum(grad * rounded.astype(jnp.float32), axis=0, keepdims=True)
+            terms = (squares / (2.0 * total_rows) - jnp.log(dv)
                      + penalty * jnp.sum(jnp.abs(wd) + jnp.abs(wo), axis=0, keepdims=True))
             acc[step:step + 1, :] += terms
-            low = product.astype(jnp.bfloat16)
-            gd = lax.dot_general(a, low, over_first, preferred_element_type=jnp.float32) / total_rows
-            go = lax.dot_general(b, low, over_first, preferred_element_type=jnp.float32) / total_rows
+            grad = grad / total_rows
+            gd, go = grad[:width], grad[width:]
             wo = shrink(wo - step_length * go, step_length * penalty)
             wd = jnp.where(eye, 0.0, shrink(wd - step_length * gd, step_length * penalty))
             along = jnp.sum(jnp.where(eye, gd, 0.0), axis=0, keepdims=True)
@@ -156,18 +181,17 @@
             out_copy(d, i).start()
 
     acc[...] = jnp.zeros_like(acc)
-    z_local().start()
-    lax.fori_loop(1, var, lambda i, c: (z_copy(i).start(), c)[1], 0)
-    start_near(0)
-    z_local().wait()
-    forward(0)
-    lax.fori_loop(1, var, lambda i, c: (start_near(i), c)[1], 0)
+    for i in range(1, var):
+        z_copy(i).start()
+    start_cc(0)
+    start_oo(0, lambda u, k: far_ref[v, k])
+    lax.fori_loop(1, var, lambda i, c: (start_cc(i), c)[1], 0)
 
     def turn(i, carry):
         @pl.when(i < var)
         def _():
             z_copy(i).wait_recv()
-            forward(i)
+            start_oo(i, lambda u, k: farz[u, k])
 
         column(i - 1)
         return carry
@@ -177,15 +201,11 @@
     tails_ref[s, var:, :] = acc[...]
 
     def tail_copy(d):
-        return pltpu.make_async_remote_copy(
-            src_ref=tails_ref.at[s], dst_ref=tails_ref.at[s],
-            send_sem=tail_s.at[d], recv_sem=tail_r.at[d],
-            device_id={"samp": flip(s, d, samp)}, device_id_type=MESH)
+        return remote(tails_ref.at[s], tails_ref.at[s], tail_s.at[d], tail_r.at[d],
+                      samp=flip(s, d, samp))
 
     def oz_copy(i):
-        return pltpu.make_async_remote_copy(
-            src_ref=oz.at[v], dst_ref=oz.at[v], send_sem=oz_s.at[i], recv_sem=oz_r.at[i],
-            device_id={"var": flip(v, i, var)}, device_id_type=MESH)
+        return remote(oz.at[v], oz.at[v], oz_s.at[i], oz_r.at[i], var=flip(v, i, var))
 
     for d in range(1, samp):
         tail_copy(d).start()
@@ -206,8 +226,8 @@
 
     def finish(i, carry):
         for d in range(1, samp):
-            near_copy(d, i).wait_send()
-            fwd_copy(d, i).wait_send()
+            cc_copy(d, i).wait_send()
+            oo_copy(d, i).wait_send()
             out_copy(d, i).wait()
         return carry
 
@@ -247,44 +267,57 @@
     wanted = jnp.sum(jnp.where(match, resident[:, None], 0), axis=0)
     near_idx = jnp.sum(jnp.where(match, ids[:, None], 0), axis=0)
     own_slot = jnp.sum(jnp.where(match, diag_slot[:, None], 0), axis=0)
-    asked = lax.all_to_all(wanted, "var", split_axis=0, concat_axis=0, tiled=True)
+    want = jnp.pad(wanted.reshape(var, 1, samp), ((0, 0), (0, 0), (0, width - samp)))
 
     vmem = pl.BlockSpec(memory_space=pltpu.VMEM)
     smem = pl.BlockSpec(memory_space=pltpu.SMEM)
     hbm = pl.BlockSpec(memory_space=pl.ANY)
+    dma = pltpu.SemaphoreType.DMA
+    bf16, f32 = jnp.bfloat16, jnp.float32
+    asked = pl.pallas_call(
+        functools.partial(ask_kernel, var),
+        out_shape=jax.ShapeDtypeStruct((var, 1, width), jnp.int32),
+        in_specs=[vmem],
+        out_specs=vmem,
+        scratch_shapes=[pltpu.VMEM((var, 1, width), jnp.int32), dma((var,)), dma((var,))],
+        compiler_params=pltpu.CompilerParams(collective_id=1, has_side_effects=True),
+        name="ask",
+    )(want)
     near, far, own, own_dia = pl.pallas_call(
         functools.partial(pack_kernel, samp, var),
         out_shape=(
             jax.ShapeDtypeStruct((samp, var, rows, width), observed.dtype),
             jax.ShapeDtypeStruct((var, samp, rows, width), observed.dtype),
-            jax.ShapeDtypeStruct((var, 2, width, width), jnp.float32),
-            jax.ShapeDtypeStruct((var, width), jnp.float32),
+            jax.ShapeDtypeStruct((var, 2, width, width), f32),
+            jax.ShapeDtypeStruct((var, width), f32),
         ),
         in_specs=[smem, smem, smem, vmem, hbm, vmem],
         out_specs=(vmem,) * 4,
-        scratch_shapes=[pltpu.SemaphoreType.DMA((var, 2))],
+        scratch_shapes=[dma((var, 2))],
         name="pack",
     )(near_idx, asked, own_slot, observed, blocks, diagonal.reshape(cols, width))
-
-    dma = pltpu.SemaphoreType.DMA
     fin, tails, whole = pl.pallas_call(
         functools.partial(main_kernel, samp, var),
         out_shape=(
-            jax.ShapeDtypeStruct((samp, var, 2, width, width), jnp.bfloat16),
-            jax.ShapeDtypeStruct((samp, var + 8, width), jnp.float32),
-            jax.ShapeDtypeStruct((8, width), jnp.float32),
+            jax.ShapeDtypeStruct((samp, var, 2, width, width), bf16),
+            jax.ShapeDtypeStruct((samp, var + 8, width), f32),
+            jax.ShapeDtypeStruct((8, width), f32),
         ),
         in_specs=[vmem] * 4,
         out_specs=(vmem,) * 3,
         scratch_shapes=[
-            pltpu.VMEM((samp, var, rows, width), observed.dtype),
             pltpu.VMEM((var, samp, rows, width), observed.dtype),
-            pltpu.VMEM((var, samp, rows, width), observed.dtype),
-            pltpu.VMEM((var, 8, width), jnp.float32),
-            pltpu.VMEM((8, width), jnp.float32),
+            pltpu.VMEM((var, samp, width, width), bf16),
+            pltpu.VMEM((var, samp, width, width), bf16),
+            pltpu.VMEM((var, width, width), f32),
+            pltpu.VMEM((var, samp, width, 2 * width), bf16),
+            pltpu.VMEM((var, samp, width, 2 * width), bf16),
+            pltpu.VMEM((var, width, 2 * width), f32),
+            pltpu.VMEM((var, 8, width), f32),
+            pltpu.VMEM((8, width), f32),
             dma((samp, var)), dma((samp, var)), dma((var,)), dma((var,)),
             dma((samp, var)), dma((samp, var)), dma((samp, var)), dma((samp, var)),
-            dma((var,)), dma((var,)), dma, dma((samp,)), dma((samp,)), dma((var,)), dma((var,)),
+            dma((samp,)), dma((samp,)), dma((var,)), dma((var,)),
         ],
         compiler_params=pltpu.CompilerParams(collective_id=0, has_side_effects=True),
         name="columns",

time: 112 us -> 97 us (0.87)
  blocking collectives: 11.7 us -> 0 us
  Pallas kernels: 93.8 us -> 91.7 us
    all_to_all x1 -> x0, blocking collectives: 11.7 us -> none  [column_body(): lax.all_to_all(wanted, 'var', split_axis=0, concat_axis=0, tiled=True)]
    pallas_call x1, Pallas kernels: 83.3 us -> 72.6 us  [column_body(): pl.pallas_call(functools.partial(main_kernel, samp, var), out_shape=(jax....]
    pallas_call x0 -> x1, Pallas kernels: none -> 8.63 us  [column_body(): pl.pallas_call(functools.partial(ask_kernel, var), out_shape=jax.ShapeDty...]
    all_to_all x3 -> x0, local copies, waits for them, and re-layouts: 1.25 us -> none  [column_body(): lax.all_to_all(wanted, 'var', split_axis=0, concat_axis=0, tiled=True)]
where the time goes in v2:
time: 97 us; the launch traced here: 96.7 us
  Pallas kernels  91.7 us (95%)
  other arithmetic  3.53 us (4%)
    pallas_call x1, Pallas kernels, column_body(): pl.pallas_call(functools.partial(main_kernel, samp, var), out_shape=(jax....  72.6 us
    pallas_call x1, Pallas kernels, column_body(): pl.pallas_call(functools.partial(ask_kernel, var), out_shape=jax.ShapeDty...  8.63 us
    pallas_call x1, Pallas kernels, column_body(): pl.pallas_call(functools.partial(pack_kernel, samp, var), out_shape=(jax....  5.36 us
    pallas_call x1, Pallas kernels, column_body(): pl.pallas_call(functools.partial(unpack_kernel, group), out_shape=(jax.Sh...  5.15 us

profile of v2, /device:TPU:0, one launch (start us, length us, event | category | flops | bytes accessed | tf_op | source)
XLA Modules:
  0.0 96.7 jit_solution(15965803354612617363)
XLA Ops:
  0.6 0.7 select_reduce_fusion.3
  1.3 0.7 broadcast_compare_fusion
  2.0 0.0 copy-start
  2.1 0.0 copy-start.1
  2.1 0.2 convert_reduce_fusion.rank
  2.3 0.0 copy-start.2
  2.3 0.6 select_reduce_fusion
  2.9 0.1 reshape.75
  3.0 0.6 pad.4.want_ref
  3.6 8.6 %ask.1.far_idx = s32[8,1,128]{2,1,0:T(1,128)} custom-call(s32[8,1,128]{2,1,0:T(1,128)} %pad.4.want_ref), custom_call_target="tpu_custom_call" | custom-call | tf_op jit(solution)/shard_map/ask/pallas_call | solution.py:277
  12.2 5.4 %pack.1 = (bf16[4,8,256,128]{3,2,1,0:T(8,128)(2,1)}, bf16[8,4,256,128]{3,2,1,0:T(8,128)(2,1)}, f32[8,2,128,128]{3,2,1,0:T(8,128)}, f32[8,128]{1,0:T(8,128)}) custom-call(s32[32]{0:T(128)} %get-tuple-element.23.near_idx, s32[8,1,128]{2,1,0:T(1,128)} %ask.1.far_idx, s32[32]{0:T(128)} %get-tuple-element.21.own_slot, bf16[256,4096]{1,0:T(8,128)(2,1)} %x_ref.1, ...), custom_call_target="tpu_custom_call" | custom-call | tf_op jit(solution)/shard_map/pack/pallas_call | solution.py:286
  17.6 0.0 copy-done
  17.6 0.0 copy-done.1
  17.6 0.0 copy-done.2
  17.6 72.6 %columns.1 = (bf16[4,8,2,128,128]{4,3,2,1,0:T(8,128)(2,1)}, f32[4,16,128]{2,1,0:T(8,128)}, f32[8,128]{1,0:T(8,128)}) custom-call(bf16[4,8,256,128]{3,2,1,0:T(8,128)(2,1)} %get-tuple-element.12.near_ref, bf16[8,4,256,128]{3,2,1,0:T(8,128)(2,1)} %get-tuple-element.13.far_ref, f32[8,2,128,128]{3,2,1,0:T(8,128)} %get-tuple-element.14.blk_ref, ...), custom_call_target="tpu_custom_call" | custom-call | tf_op jit(solution)/shard_map/columns/pallas_call | solution.py:299
  90.2 0.8 slice_reduce_fusion
  91.0 0.5 broadcast_multiply_fusion
  91.5 5.1 %unpack.1 = (f32[32,2,128,128]{3,2,1,0:T(8,128)}, f32[32,128]{1,0:T(8,128)}) custom-call(s32[32]{0:T(128)} %copy-done.1, s32[32]{0:T(128)} %copy-done.2, s32[32]{0:T(128)} %copy-done, bf16[4,8,2,128,128]{4,3,2,1,0:T(8,128)(2,1)} %get-tuple-element.16.fin_ref, f32[4,16,128]{2,1,0:T(8,128)} %get-tuple-element.17.tails_ref), custom_call_target="tpu_custom_call" | custom-call | tf_op jit(solution)/shard_map/unpack/pallas_call | solution.py:327
  (4 shorter events, 0.0 us)
Async XLA Ops:
  2.0 15.6 %copy-start = (s32[32]{0:T(128)}, s32[32]{0:T(128)S(1)}, u32[]{:S(2)}) copy-start(s32[32]{0:T(128)S(1)} %fusion.1.slot) | copy-start | bytes 388
  2.1 15.6 %copy-start.1 = (s32[32]{0:T(128)}, s32[32]{0:T(128)S(1)}, u32[]{:S(2)}) copy-start(s32[32]{0:T(128)S(1)} %get-tuple-element.25.owner) | copy-start | bytes 388
  2.3 15.4 %copy-start.2 = (s32[32]{0:T(128)}, s32[32]{0:T(128)S(1)}, u32[]{:S(2)}) copy-start(s32[32]{0:T(128)S(1)} %convert_reduce_fusion.rank) | copy-start | bytes 388

commit v3 on v2

--- a/solution.py
+++ b/solution.py
@@ -27,60 +27,26 @@
     return out
 
 
-def ask_kernel(var, want_ref, asked_ref, got, send, recv):
-    v = lax.axis_index("var")
-    barrier = pltpu.get_barrier_semaphore()
-    for i in range(1, var):
-        pl.semaphore_signal(barrier, inc=1, device_id={"var": flip(v, i, var)}, device_id_type=MESH)
-    pl.semaphore_wait(barrier, var - 1)
-
-    def copy(i):
-        u = flip(v, i, var)
-        return pltpu.make_async_remote_copy(
-            src_ref=want_ref.at[u], dst_ref=got.at[v], send_sem=send.at[i], recv_sem=recv.at[i],
-            device_id={"var": u}, device_id_type=MESH)
-
-    for i in range(1, var):
-        copy(i).start()
-    got[v] = want_ref[v]
-    for i in range(1, var):
-        copy(i).wait()
-    asked_ref[...] = got[...]
-
-
-def pack_kernel(samp, var, near_idx, far_idx, own_slot, x_ref, blk_hbm, dia_ref,
-                near_ref, far_ref, own_ref, odia_ref, sem):
-    width = dia_ref.shape[1]
-    me = lax.axis_index("samp")
-    copies = []
-    for u in range(var):
-        col = near_idx[u * samp + me]
-        slot = own_slot[u * samp + me]
-        for part in range(2):
-            which = slot if part == 0 else 1 - slot
-            copy = pltpu.make_async_copy(blk_hbm.at[col, which], own_ref.at[u, part], sem.at[u, part])
-            copy.start()
-            copies.append(copy)
-        odia_ref[pl.ds(u, 1), :] = dia_ref[pl.ds(col, 1), :]
-    for u in range(var):
-        for k in range(samp):
-            at = u * samp + k
-            near = pl.multiple_of(near_idx[at] * width, width)
-            near_ref[k, u] = x_ref[:, pl.ds(near, width)]
-            far = pl.multiple_of(far_idx[u, 0, k] * width, width)
-            far_ref[u, k] = x_ref[:, pl.ds(far, width)]
-    for copy in copies:
-        copy.wait()
-
-
-def main_kernel(samp, var, near_ref, far_ref, blk_ref, dia_ref, fin_ref, tails_ref, obj_ref, farz, cc_out, cc_in, cc_own, oo_out, oo_in, oo_own, oz, acc,
-                cc_s, cc_r, z_s, z_r, oo_s, oo_r, out_s, out_r,
+def main_kernel(samp, var, near_idx, wanted, own_slot, want_ref, x_hbm, blk_hbm, dia_ref,
+                fin_ref, tails_ref, obj_ref,
+                x, blk, ask, ask_s, far, farz, cc_out, cc_in, cc_own, oo_out, oo_in, oo_own, oz, acc,
+                load, ask_ss, ask_rs, ask_l, cc_s, cc_r, z_s, z_r, oo_s, oo_r, out_s, out_r,
                 tail_s, tail_r, oz_s, oz_r):
     s = lax.axis_index("samp")
     v = lax.axis_index("var")
-    rows, width = farz.shape[2], farz.shape[3]
+    rows, width = x.shape[1], x.shape[2]
     total_rows = rows * samp
     over_first = (((0,), (0,)), ((), ()))
+
+    cols = x.shape[0]
+    x_loads = [
+        pltpu.make_async_copy(x_hbm.at[:, l * width:(l + 1) * width], x.at[l], load.at[l])
+        for l in range(cols)
+    ]
+    for x_load in x_loads:
+        x_load.start()
+    blk_load = pltpu.make_async_copy(blk_hbm, blk, load.at[cols])
+    blk_load.start()
 
     barrier = pltpu.get_barrier_semaphore()
     for i in range(1, var):
@@ -94,9 +60,13 @@
             src_ref=src, dst_ref=dst, send_sem=send, recv_sem=recv,
             device_id=where, device_id_type=MESH)
 
+    def ask_copy(i):
+        u = flip(v, i, var)
+        return remote(want_ref.at[u], ask.at[v], ask_ss.at[i], ask_rs.at[i], var=u)
+
     def z_copy(i):
         u = flip(v, i, var)
-        return remote(far_ref.at[u], farz.at[v], z_s.at[i], z_r.at[i], var=u)
+        return remote(far.at[u], farz.at[v], z_s.at[i], z_r.at[i], var=u)
 
     def cc_copy(d, i):
         u, k = flip(v, i, var), flip(s, d, samp)
@@ -110,19 +80,37 @@
         u, k = flip(v, i, var), flip(s, d, samp)
         return remote(fin_ref.at[s, u], fin_ref.at[s, u], out_s.at[d, i], out_r.at[d, i], samp=k)
 
+    def panel(index):
+        return x[index]
+
+    def near_panel(u, k):
+        return panel(near_idx[u * samp + k])
+
     def gram(left, right):
         return lax.dot_general(left, right, over_first, preferred_element_type=jnp.float32)
 
+    eye = lax.broadcasted_iota(jnp.int32, (width, width), 0) == lax.broadcasted_iota(
+        jnp.int32, (width, width), 1)
+
+    def residual(part):
+        off = jnp.where(eye, part - part.astype(jnp.bfloat16).astype(jnp.float32), 0.0)
+        row = jnp.sum(off, axis=0, keepdims=True)
+        return jnp.broadcast_to(row, (16, width)).astype(jnp.bfloat16)
+
+    def restored(block, rest):
+        return block.astype(jnp.float32) + jnp.where(eye, rest.astype(jnp.float32)[:1], 0.0)
+
     def start_cc(i):
         u = flip(v, i, var)
         for d in range(samp):
             k = flip(s, d, samp)
-            c = near_ref[k, u]
+            c = near_panel(u, k)
             part = gram(c, c)
             if d == 0:
                 cc_own[u] = part
             else:
-                cc_out[u, k] = part.astype(jnp.bfloat16)
+                cc_out[u, k, :width] = part.astype(jnp.bfloat16)
+                cc_out[u, k, width:] = residual(part)
                 cc_copy(d, i).start()
 
     def start_oo(i, far_panel):
@@ -130,34 +118,36 @@
         for d in range(samp):
             k = flip(s, d, samp)
             o = far_panel(u, k)
-            part = gram(o, jnp.concatenate([near_ref[k, u], o], axis=1))
+            part = gram(o, jnp.concatenate([near_panel(u, k), o], axis=1))
             if d == 0:
                 oo_own[u] = part
             else:
-                oo_out[u, k] = part.astype(jnp.bfloat16)
+                oo_out[u, k, :width] = part.astype(jnp.bfloat16)
+                rest = residual(part[:, width:])
+                oo_out[u, k, width:] = jnp.concatenate([rest, rest], axis=1)
                 oo_copy(d, i).start()
-
-    eye = lax.broadcasted_iota(jnp.int32, (width, width), 0) == lax.broadcasted_iota(
-        jnp.int32, (width, width), 1)
 
     def column(i):
         u = flip(v, i, var)
         for d in range(1, samp):
             cc_copy(d, i).wait_recv()
             oo_copy(d, i).wait_recv()
-        cc, oo = cc_own[u], oo_own[u]
+        cc, oc, oo = cc_own[u], oo_own[u, :, :width], oo_own[u, :, width:]
         for d in range(1, samp):
             p = flip(s, d, samp)
-            cc = cc + cc_in[u, p].astype(jnp.float32)
-            oo = oo + oo_in[u, p].astype(jnp.float32)
+            cc = cc + restored(cc_in[u, p, :width], cc_in[u, p, width:])
+            oc = oc + oo_in[u, p, :width, :width].astype(jnp.float32)
+            oo = oo + restored(oo_in[u, p, :width, width:], oo_in[u, p, width:, width:])
         both = jnp.concatenate(
-            [jnp.concatenate([cc, oo[:, :width].T], axis=1), oo], axis=0)
+            [jnp.concatenate([cc, oc.T], axis=1), jnp.concatenate([oc, oo], axis=1)], axis=0)
         high = both.astype(jnp.bfloat16)
         low = (both - high.astype(jnp.float32)).astype(jnp.bfloat16)
         gram_parts = jnp.concatenate([high, low], axis=1)
-        wd = jnp.where(eye, 0.0, blk_ref[u, 0])
-        wo = blk_ref[u, 1]
-        dv = dia_ref[pl.ds(u, 1), :]
+        col = near_idx[u * samp + s]
+        slot = own_slot[u * samp + s]
+        wd = jnp.where(eye, 0.0, blk[col, slot])
+        wo = blk[col, 1 - slot]
+        dv = dia_ref[col]
         for step in range(STEPS):
             rounded = jnp.concatenate(
                 [jnp.where(eye, dv, wd).astype(jnp.bfloat16), wo.astype(jnp.bfloat16)], axis=0)
@@ -180,12 +170,30 @@
         for d in range(1, samp):
             out_copy(d, i).start()
 
+    for i in range(1, var):
+        ask_copy(i).start()
     acc[...] = jnp.zeros_like(acc)
-    for i in range(1, var):
+    for x_load in x_loads:
+        x_load.wait()
+    start_cc(0)
+    for i in range(1, var):
+        ask_copy(i).wait_recv()
+    ask[v] = want_ref[v]
+    ask_load = pltpu.make_async_copy(ask, ask_s, ask_l)
+    ask_load.start()
+    ask_load.wait()
+
+    def send_far(i, carry):
+        u = flip(v, i, var)
+        for k in range(samp):
+            far[u, k] = panel(ask_s[u, 0, k])
         z_copy(i).start()
-    start_cc(0)
-    start_oo(0, lambda u, k: far_ref[v, k])
+        return carry
+
+    lax.fori_loop(1, var, send_far, 0)
+    start_oo(0, lambda u, k: panel(wanted[u * samp + k]))
     lax.fori_loop(1, var, lambda i, c: (start_cc(i), c)[1], 0)
+    blk_load.wait()
 
     def turn(i, carry):
         @pl.when(i < var)
@@ -235,6 +243,7 @@
     for d in range(1, samp):
         tail_copy(d).wait_send()
     for i in range(1, var):
+        ask_copy(i).wait_send()
         z_copy(i).wait_send()
         oz_copy(i).wait_send()
 
@@ -274,28 +283,6 @@
     hbm = pl.BlockSpec(memory_space=pl.ANY)
     dma = pltpu.SemaphoreType.DMA
     bf16, f32 = jnp.bfloat16, jnp.float32
-    asked = pl.pallas_call(
-        functools.partial(ask_kernel, var),
-        out_shape=jax.ShapeDtypeStruct((var, 1, width), jnp.int32),
-        in_specs=[vmem],
-        out_specs=vmem,
-        scratch_shapes=[pltpu.VMEM((var, 1, width), jnp.int32), dma((var,)), dma((var,))],
-        compiler_params=pltpu.CompilerParams(collective_id=1, has_side_effects=True),
-        name="ask",
-    )(want)
-    near, far, own, own_dia = pl.pallas_call(
-        functools.partial(pack_kernel, samp, var),
-        out_shape=(
-            jax.ShapeDtypeStruct((samp, var, rows, width), observed.dtype),
-            jax.ShapeDtypeStruct((var, samp, rows, width), observed.dtype),
-            jax.ShapeDtypeStruct((var, 2, width, width), f32),
-            jax.ShapeDtypeStruct((var, width), f32),
-        ),
-        in_specs=[smem, smem, smem, vmem, hbm, vmem],
-        out_specs=(vmem,) * 4,
-        scratch_shapes=[dma((var, 2))],
-        name="pack",
-    )(near_idx, asked, own_slot, observed, blocks, diagonal.reshape(cols, width))
     fin, tails, whole = pl.pallas_call(
         functools.partial(main_kernel, samp, var),
         out_shape=(
@@ -303,25 +290,31 @@
             jax.ShapeDtypeStruct((samp, var + 8, width), f32),
             jax.ShapeDtypeStruct((8, width), f32),
         ),
-        in_specs=[vmem] * 4,
+        in_specs=[smem, smem, smem, vmem, hbm, hbm, vmem],
         out_specs=(vmem,) * 3,
         scratch_shapes=[
+            pltpu.VMEM((cols, rows, width), observed.dtype),
+            pltpu.VMEM(blocks.shape, f32),
+            pltpu.VMEM((var, 1, width), jnp.int32),
+            pltpu.SMEM((var, 1, width), jnp.int32),
             pltpu.VMEM((var, samp, rows, width), observed.dtype),
-            pltpu.VMEM((var, samp, width, width), bf16),
-            pltpu.VMEM((var, samp, width, width), bf16),
+            pltpu.VMEM((var, samp, rows, width), observed.dtype),
+            pltpu.VMEM((var, samp, width + 16, width), bf16),
+            pltpu.VMEM((var, samp, width + 16, width), bf16),
             pltpu.VMEM((var, width, width), f32),
-            pltpu.VMEM((var, samp, width, 2 * width), bf16),
-            pltpu.VMEM((var, samp, width, 2 * width), bf16),
+            pltpu.VMEM((var, samp, width + 16, 2 * width), bf16),
+            pltpu.VMEM((var, samp, width + 16, 2 * width), bf16),
             pltpu.VMEM((var, width, 2 * width), f32),
             pltpu.VMEM((var, 8, width), f32),
             pltpu.VMEM((8, width), f32),
+            dma((cols + 1,)), dma((var,)), dma((var,)), dma,
             dma((samp, var)), dma((samp, var)), dma((var,)), dma((var,)),
             dma((samp, var)), dma((samp, var)), dma((samp, var)), dma((samp, var)),
             dma((samp,)), dma((samp,)), dma((var,)), dma((var,)),
         ],
         compiler_params=pltpu.CompilerParams(collective_id=0, has_side_effects=True),
         name="columns",
-    )(near, far, own, own_dia)
+    )(near_idx, wanted, own_slot, want, observed, blocks, diagonal.reshape(cols, 1, width))
 
     group = 4
     new_blocks, new_diagonal = pl.pallas_call(

time: 97 us -> 91.2 us (0.940)
  Pallas kernels: 91.7 us -> 86 us
    pallas_call x2 -> x0, Pallas kernels: 14 us -> none  [the longest x1 8.63 us: column_body(): pl.pallas_call(functools.partial(ask_kernel, var), out_shape=jax.ShapeDty...]
    pallas_call x1, Pallas kernels: 72.6 us -> 80.8 us  [column_body(): pl.pallas_call(functools.partial(main_kernel, samp, var), out_shape=(jax....]
where the time goes in v3:
time: 91.2 us; the launch traced here: 90.9 us
  Pallas kernels  86 us (94%)
  other arithmetic  3.51 us (4%)
    pallas_call x1, Pallas kernels, column_body(): pl.pallas_call(functools.partial(main_kernel, samp, var), out_shape=(jax....  80.8 us
    pallas_call x1, Pallas kernels, column_body(): pl.pallas_call(functools.partial(unpack_kernel, group), out_shape=(jax.Sh...  5.18 us

profile of v3, /device:TPU:0, one launch (start us, length us, event | category | flops | bytes accessed | tf_op | source)
XLA Modules:
  0.0 90.9 jit_solution(14659813917063144139)
XLA Ops:
  0.6 0.7 select_reduce_fusion.3
  1.3 0.7 broadcast_compare_fusion
  2.0 0.0 copy-start.1
  2.1 0.0 copy-start.2
  2.1 0.2 convert_reduce_fusion.rank
  2.3 0.0 copy-start.3
  2.3 0.6 select_reduce_fusion
  2.9 0.0 copy-start
  2.9 0.1 reshape.75
  3.0 0.6 pad.4.want_ref
  3.6 0.0 copy-done
  3.6 80.8 %columns.1 = (bf16[4,8,2,128,128]{4,3,2,1,0:T(8,128)(2,1)}, f32[4,16,128]{2,1,0:T(8,128)}, f32[8,128]{1,0:T(8,128)}) custom-call(s32[32]{0:T(128)} %get-tuple-element.15.near_idx, s32[32]{0:T(128)} %copy-done, s32[32]{0:T(128)} %get-tuple-element.13.own_slot, s32[8,1,128]{2,1,0:T(1,128)} %pad.4.want_ref, bf16[256,4096]{1,0:T(8,128)(2,1)} %x_hbm.1, ...), custom_call_target="tpu_custom_call" | custom-call | tf_op jit(solution)/shard_map/columns/pallas_call | solution.py:286
  84.4 0.8 slice_reduce_fusion
  85.2 0.5 broadcast_multiply_fusion
  85.7 0.0 copy-done.1
  85.7 0.0 copy-done.2
  85.7 0.0 copy-done.3
  85.7 5.2 %unpack.1 = (f32[32,2,128,128]{3,2,1,0:T(8,128)}, f32[32,128]{1,0:T(8,128)}) custom-call(s32[32]{0:T(128)} %copy-done.2, s32[32]{0:T(128)} %copy-done.3, s32[32]{0:T(128)} %copy-done.1, bf16[4,8,2,128,128]{4,3,2,1,0:T(8,128)(2,1)} %get-tuple-element.8.fin_ref, f32[4,16,128]{2,1,0:T(8,128)} %get-tuple-element.9.tails_ref), custom_call_target="tpu_custom_call" | custom-call | tf_op jit(solution)/shard_map/unpack/pallas_call | solution.py:320
  (4 shorter events, 0.0 us)
Async XLA Ops:
  2.0 83.7 %copy-start.1 = (s32[32]{0:T(128)}, s32[32]{0:T(128)S(1)}, u32[]{:S(2)}) copy-start(s32[32]{0:T(128)S(1)} %fusion.1.slot) | copy-start | bytes 388
  2.1 83.7 %copy-start.2 = (s32[32]{0:T(128)}, s32[32]{0:T(128)S(1)}, u32[]{:S(2)}) copy-start(s32[32]{0:T(128)S(1)} %get-tuple-element.17.owner) | copy-start | bytes 388
  2.3 83.5 %copy-start.3 = (s32[32]{0:T(128)}, s32[32]{0:T(128)S(1)}, u32[]{:S(2)}) copy-start(s32[32]{0:T(128)S(1)} %convert_reduce_fusion.rank) | copy-start | bytes 388
  2.9 0.7 copy-start

commit v4 on v3

--- a/solution.py
+++ b/solution.py
@@ -31,7 +31,7 @@
                 fin_ref, tails_ref, obj_ref,
                 x, blk, ask, ask_s, far, farz, cc_out, cc_in, cc_own, oo_out, oo_in, oo_own, oz, acc,
                 load, ask_ss, ask_rs, ask_l, cc_s, cc_r, z_s, z_r, oo_s, oo_r, out_s, out_r,
-                tail_s, tail_r, oz_s, oz_r):
+                rel_s, rel_r, tail_s, tail_r, oz_s, oz_r):
     s = lax.axis_index("samp")
     v = lax.axis_index("var")
     rows, width = x.shape[1], x.shape[2]
@@ -92,13 +92,26 @@
     eye = lax.broadcasted_iota(jnp.int32, (width, width), 0) == lax.broadcasted_iota(
         jnp.int32, (width, width), 1)
 
-    def residual(part):
+    row_at = lax.broadcasted_iota(jnp.int32, (width, width), 0)
+    col_at = lax.broadcasted_iota(jnp.int32, (width, width), 1)
+    spare = (row_at == col_at + 1) | ((row_at == width - 1) & (col_at == 0))
+
+    def rounded_symmetric(part):
         off = jnp.where(eye, part - part.astype(jnp.bfloat16).astype(jnp.float32), 0.0)
         row = jnp.sum(off, axis=0, keepdims=True)
-        return jnp.broadcast_to(row, (16, width)).astype(jnp.bfloat16)
-
-    def restored(block, rest):
-        return block.astype(jnp.float32) + jnp.where(eye, rest.astype(jnp.float32)[:1], 0.0)
+        below = jnp.where(row_at == col_at + 1, row, part)
+        corner = jnp.where((row_at == width - 1) & (col_at == 0), row[:, width - 1:], below)
+        return corner.astype(jnp.bfloat16)
+
+    def own_symmetric(part):
+        return jnp.where(spare, 0.0, part)
+
+    def restored(total):
+        below = jnp.where(row_at == col_at + 1, total, 0.0)
+        row = jnp.sum(below, axis=0, keepdims=True)
+        last = total[width - 1:, :1]
+        row = jnp.where(col_at[:1] == width - 1, last, row)
+        return jnp.where(spare, total.T, total) + jnp.where(eye, row, 0.0)
 
     def start_cc(i):
         u = flip(v, i, var)
@@ -107,10 +120,9 @@
             c = near_panel(u, k)
             part = gram(c, c)
             if d == 0:
-                cc_own[u] = part
+                cc_own[u] = own_symmetric(part)
             else:
-                cc_out[u, k, :width] = part.astype(jnp.bfloat16)
-                cc_out[u, k, width:] = residual(part)
+                cc_out[u, k] = rounded_symmetric(part)
                 cc_copy(d, i).start()
 
     def start_oo(i, far_panel):
@@ -120,11 +132,11 @@
             o = far_panel(u, k)
             part = gram(o, jnp.concatenate([near_panel(u, k), o], axis=1))
             if d == 0:
-                oo_own[u] = part
+                oo_own[u, :, :width] = part[:, :width]
+                oo_own[u, :, width:] = own_symmetric(part[:, width:])
             else:
-                oo_out[u, k, :width] = part.astype(jnp.bfloat16)
-                rest = residual(part[:, width:])
-                oo_out[u, k, width:] = jnp.concatenate([rest, rest], axis=1)
+                oo_out[u, k, :, :width] = part[:, :width].astype(jnp.bfloat16)
+                oo_out[u, k, :, width:] = rounded_symmetric(part[:, width:])
                 oo_copy(d, i).start()
 
     def column(i):
@@ -135,9 +147,10 @@
         cc, oc, oo = cc_own[u], oo_own[u, :, :width], oo_own[u, :, width:]
         for d in range(1, samp):
             p = flip(s, d, samp)
-            cc = cc + restored(cc_in[u, p, :width], cc_in[u, p, width:])
-            oc = oc + oo_in[u, p, :width, :width].astype(jnp.float32)
-            oo = oo + restored(oo_in[u, p, :width, width:], oo_in[u, p, width:, width:])
+            cc = cc + cc_in[u, p].astype(jnp.float32)
+            oc = oc + oo_in[u, p, :, :width].astype(jnp.float32)
+            oo = oo + oo_in[u, p, :, width:].astype(jnp.float32)
+        cc, oo = restored(cc), restored(oo)
         both = jnp.concatenate(
             [jnp.concatenate([cc, oc.T], axis=1), jnp.concatenate([oc, oo], axis=1)], axis=0)
         high = both.astype(jnp.bfloat16)
@@ -167,8 +180,21 @@
         fin_ref[s, u, 0] = wd.astype(jnp.bfloat16)
         fin_ref[s, u, 1] = wo.astype(jnp.bfloat16)
         tails_ref[s, pl.ds(u, 1), :] = dv
-        for d in range(1, samp):
+
+    def send_out(i, direct):
+        for d in range(1, samp if direct else samp - 1):
             out_copy(d, i).start()
+
+    def relay_copy(part, i):
+        u = flip(v, i, var)
+        near, to = flip(s, 1 + part, samp), flip(s, 2 - part, samp)
+        return remote(fin_ref.at[near, u, part], fin_ref.at[near, u, part],
+                      rel_s.at[part, i], rel_r.at[part, i], samp=to)
+
+    def relay(i):
+        for part in range(2):
+            out_copy(1 + part, i).wait_recv()
+            relay_copy(part, i).start()
 
     for i in range(1, var):
         ask_copy(i).start()
@@ -202,6 +228,19 @@
             start_oo(i, lambda u, k: farz[u, k])
 
         column(i - 1)
+
+        @pl.when(i < var - 1)
+        def _():
+            send_out(i - 1, False)
+
+        @pl.when(i == var - 1)
+        def _():
+            send_out(i - 1, True)
+
+        @pl.when(i > 2)
+        def _():
+            relay(i - 3)
+
         return carry
 
     lax.fori_loop(1, var + 1, turn, 0)
@@ -217,6 +256,7 @@
 
     for d in range(1, samp):
         tail_copy(d).start()
+    send_out(var - 1, True)
     for d in range(1, samp):
         tail_copy(d).wait_recv()
     group = tails_ref[0, var:, :]
@@ -236,10 +276,21 @@
         for d in range(1, samp):
             cc_copy(d, i).wait_send()
             oo_copy(d, i).wait_send()
-            out_copy(d, i).wait()
+        for d in range(1, samp - 1):
+            out_copy(d, i).wait_send()
         return carry
 
+    def finish_relay(i, carry):
+        for part in range(2):
+            relay_copy(part, i).wait()
+        return carry
+
     lax.fori_loop(0, var, finish, 0)
+    lax.fori_loop(0, var - 2, finish_relay, 0)
+    for i in range(var - 2, var):
+        for d in range(1, samp - 1):
+            out_copy(d, i).wait_recv()
+        out_copy(samp - 1, i).wait()
     for d in range(1, samp):
         tail_copy(d).wait_send()
     for i in range(1, var):
@@ -248,7 +299,12 @@
         oz_copy(i).wait_send()
 
 
-def unpack_kernel(group, owner, rank, slot, fin_ref, tails_ref, out_ref, dia_ref):
+def unpack_kernel(group, order, owner, rank, slot, fin_ref, tails_ref, whole_ref, out_ref, dia_ref, obj_ref):
+    @pl.when(pl.program_id(0) == 0)
+    def _():
+        for step in range(STEPS):
+            obj_ref[step] = jnp.sum(whole_ref[step:step + 1, :]) / order
+
     first = pl.program_id(0) * group
     for j in range(group):
         col = first + j
@@ -299,39 +355,40 @@
             pltpu.SMEM((var, 1, width), jnp.int32),
             pltpu.VMEM((var, samp, rows, width), observed.dtype),
             pltpu.VMEM((var, samp, rows, width), observed.dtype),
-            pltpu.VMEM((var, samp, width + 16, width), bf16),
-            pltpu.VMEM((var, samp, width + 16, width), bf16),
+            pltpu.VMEM((var, samp, width, width), bf16),
+            pltpu.VMEM((var, samp, width, width), bf16),
             pltpu.VMEM((var, width, width), f32),
-            pltpu.VMEM((var, samp, width + 16, 2 * width), bf16),
-            pltpu.VMEM((var, samp, width + 16, 2 * width), bf16),
+            pltpu.VMEM((var, samp, width, 2 * width), bf16),
+            pltpu.VMEM((var, samp, width, 2 * width), bf16),
             pltpu.VMEM((var, width, 2 * width), f32),
             pltpu.VMEM((var, 8, width), f32),
             pltpu.VMEM((8, width), f32),
             dma((cols + 1,)), dma((var,)), dma((var,)), dma,
             dma((samp, var)), dma((samp, var)), dma((var,)), dma((var,)),
             dma((samp, var)), dma((samp, var)), dma((samp, var)), dma((samp, var)),
-            dma((samp,)), dma((samp,)), dma((var,)), dma((var,)),
+            dma((2, var)), dma((2, var)), dma((samp,)), dma((samp,)), dma((var,)), dma((var,)),
         ],
         compiler_params=pltpu.CompilerParams(collective_id=0, has_side_effects=True),
         name="columns",
     )(near_idx, wanted, own_slot, want, observed, blocks, diagonal.reshape(cols, 1, width))
 
     group = 4
-    new_blocks, new_diagonal = pl.pallas_call(
-        functools.partial(unpack_kernel, group),
+    new_blocks, new_diagonal, objective = pl.pallas_call(
+        functools.partial(unpack_kernel, group, float(cols * width * var)),
         out_shape=(
             jax.ShapeDtypeStruct(blocks.shape, jnp.float32),
             jax.ShapeDtypeStruct((cols, width), jnp.float32),
+            jax.ShapeDtypeStruct((STEPS,), jnp.float32),
         ),
         grid=(cols // group,),
-        in_specs=[smem, smem, smem, vmem, vmem],
+        in_specs=[smem, smem, smem, vmem, vmem, vmem],
         out_specs=(
             pl.BlockSpec((group, 2, width, width), lambda g: (g, 0, 0, 0)),
             pl.BlockSpec((cols, width), lambda g: (0, 0)),
+            smem,
         ),
         name="unpack",
-    )(owner, rank, diag_slot, fin, tails)
-    objective = jnp.sum(whole[:STEPS], axis=1) / (cols * width * var)
+    )(owner, rank, diag_slot, fin, tails, whole)
     return new_blocks, new_diagonal.reshape(-1), objective
 
 
@@ -434,7 +491,7 @@
 def whole_body(observed, blocks, diagonal, pattern):
     cols = blocks.shape[0]
     var, samp = lax.axis_size("var"), lax.axis_size("samp")
-    exact = samp * var == cols and cols % 4 == 0 and var % 8 == 0 and blocks.shape[2] == 128
+    exact = samp == 4 and samp * var == cols and cols % 4 == 0 and var % 8 == 0 and blocks.shape[2] == 128
     if exact and power_of_two(samp) and power_of_two(var):
         return column_body(observed, blocks, diagonal, pattern)
     return body(observed, blocks, diagonal, pattern)

time: 91.2 us -> 84.4 us (0.925)
  Pallas kernels: 86 us -> 80.5 us
  other arithmetic: 3.51 us -> 2.2 us
    pallas_call x1, Pallas kernels: 80.8 us -> 75.2 us  [column_body(): pl.pallas_call(functools.partial(main_kernel, samp, var), out_shape=(jax....]
where the time goes in v4:
time: 84.4 us; the launch traced here: 84.1 us
  Pallas kernels  80.5 us (95%)
  other arithmetic  2.2 us (3%)
    pallas_call x1, Pallas kernels, column_body(): pl.pallas_call(functools.partial(main_kernel, samp, var), out_shape=(jax....  75.2 us
    pallas_call x1, Pallas kernels, column_body(): pl.pallas_call(functools.partial(unpack_kernel, group, float(cols * width...  5.35 us

profile of v4, /device:TPU:0, one launch (start us, length us, event | category | flops | bytes accessed | tf_op | source)
XLA Modules:
  0.0 84.1 jit_solution(6754643952061920409)
XLA Ops:
  0.6 0.7 select_reduce_fusion.3
  1.3 0.7 broadcast_compare_fusion
  2.0 0.0 copy-start.1
  2.1 0.0 copy-start.2
  2.1 0.2 convert_reduce_fusion.rank
  2.3 0.0 copy-start.3
  2.3 0.6 select_reduce_fusion
  2.9 0.0 copy-start
  2.9 0.1 reshape.75
  3.0 0.6 pad.4.want_ref
  3.6 0.0 copy-done
  3.6 75.2 %columns.1 = (bf16[4,8,2,128,128]{4,3,2,1,0:T(8,128)(2,1)}, f32[4,16,128]{2,1,0:T(8,128)}, f32[8,128]{1,0:T(8,128)}) custom-call(s32[32]{0:T(128)} %get-tuple-element.17.near_idx, s32[32]{0:T(128)} %copy-done, s32[32]{0:T(128)} %get-tuple-element.15.own_slot, s32[8,1,128]{2,1,0:T(1,128)} %pad.4.want_ref, bf16[256,4096]{1,0:T(8,128)(2,1)} %x_hbm.1, ...), custom_call_target="tpu_custom_call" | custom-call | tf_op jit(solution)/shard_map/columns/pallas_call | solution.py:342
  78.7 0.0 copy-done.1
  78.8 0.0 copy-done.2
  78.8 0.0 copy-done.3
  78.8 5.3 %unpack.1 = (f32[32,2,128,128]{3,2,1,0:T(8,128)}, f32[32,128]{1,0:T(8,128)}, f32[2]{0:T(128)}) custom-call(s32[32]{0:T(128)} %copy-done.2, s32[32]{0:T(128)} %copy-done.3, s32[32]{0:T(128)} %copy-done.1, bf16[4,8,2,128,128]{4,3,2,1,0:T(8,128)(2,1)} %get-tuple-element.9.fin_ref, f32[4,16,128]{2,1,0:T(8,128)} %get-tuple-element.10.tails_ref, ...), custom_call_target="tpu_custom_call" | custom-call | tf_op jit(solution)/shard_map/unpack/pallas_call | solution.py:376
  (4 shorter events, 0.0 us)
Async XLA Ops:
  2.0 76.7 %copy-start.1 = (s32[32]{0:T(128)}, s32[32]{0:T(128)S(1)}, u32[]{:S(2)}) copy-start(s32[32]{0:T(128)S(1)} %fusion.1.slot) | copy-start | bytes 388
  2.1 76.7 %copy-start.2 = (s32[32]{0:T(128)}, s32[32]{0:T(128)S(1)}, u32[]{:S(2)}) copy-start(s32[32]{0:T(128)S(1)} %get-tuple-element.19.owner) | copy-start | bytes 388
  2.3 76.5 %copy-start.3 = (s32[32]{0:T(128)}, s32[32]{0:T(128)S(1)}, u32[]{:S(2)}) copy-start(s32[32]{0:T(128)S(1)} %convert_reduce_fusion.rank) | copy-start | bytes 388
  2.9 0.7 copy-start

commit v5 on v4

--- a/solution.py
+++ b/solution.py
@@ -221,11 +221,14 @@
     lax.fori_loop(1, var, lambda i, c: (start_cc(i), c)[1], 0)
     blk_load.wait()
 
+    def take_far(i):
+        z_copy(i).wait_recv()
+        start_oo(i, lambda u, k: farz[u, k])
+
     def turn(i, carry):
-        @pl.when(i < var)
+        @pl.when(i <= var // 2)
         def _():
-            z_copy(i).wait_recv()
-            start_oo(i, lambda u, k: farz[u, k])
+            take_far(i)
 
         column(i - 1)
 
@@ -240,6 +243,10 @@
         @pl.when(i > 2)
         def _():
             relay(i - 3)
+
+        @pl.when((i > var // 2) & (i < var))
+        def _():
+            take_far(i)
 
         return carry
 

time: 84.4 us -> 88.9 us (1.053)
  Pallas kernels: 80.5 us -> 85 us
    pallas_call x1, Pallas kernels: 75.2 us -> 79.7 us  [column_body(): pl.pallas_call(functools.partial(main_kernel, samp, var), out_shape=(jax....]
where the time goes in v5:
time: 88.9 us; the launch traced here: 88.7 us
  Pallas kernels  85 us (96%)
  other arithmetic  2.2 us (2%)
    pallas_call x1, Pallas kernels, column_body(): pl.pallas_call(functools.partial(main_kernel, samp, var), out_shape=(jax....  79.7 us
    pallas_call x1, Pallas kernels, column_body(): pl.pallas_call(functools.partial(unpack_kernel, group, float(cols * width...  5.35 us

profile of v5, /device:TPU:0, one launch (start us, length us, event | category | flops | bytes accessed | tf_op | source)
XLA Modules:
  0.0 88.7 jit_solution(16203223652733405903)
XLA Ops:
  0.6 0.7 select_reduce_fusion.3
  1.3 0.7 broadcast_compare_fusion
  2.0 0.0 copy-start.1
  2.1 0.0 copy-start.2
  2.1 0.2 convert_reduce_fusion.rank
  2.3 0.0 copy-start.3
  2.3 0.6 select_reduce_fusion
  2.9 0.0 copy-start
  2.9 0.1 reshape.75
  3.0 0.6 pad.4.want_ref
  3.6 0.0 copy-done
  3.6 79.7 %columns.1 = (bf16[4,8,2,128,128]{4,3,2,1,0:T(8,128)(2,1)}, f32[4,16,128]{2,1,0:T(8,128)}, f32[8,128]{1,0:T(8,128)}) custom-call(s32[32]{0:T(128)} %get-tuple-element.17.near_idx, s32[32]{0:T(128)} %copy-done, s32[32]{0:T(128)} %get-tuple-element.15.own_slot, s32[8,1,128]{2,1,0:T(1,128)} %pad.4.want_ref, bf16[256,4096]{1,0:T(8,128)(2,1)} %x_hbm.1, ...), custom_call_target="tpu_custom_call" | custom-call | tf_op jit(solution)/shard_map/columns/pallas_call | solution.py:349
  83.3 0.0 copy-done.1
  83.3 0.0 copy-done.2
  83.3 0.0 copy-done.3
  83.3 5.3 %unpack.1 = (f32[32,2,128,128]{3,2,1,0:T(8,128)}, f32[32,128]{1,0:T(8,128)}, f32[2]{0:T(128)}) custom-call(s32[32]{0:T(128)} %copy-done.2, s32[32]{0:T(128)} %copy-done.3, s32[32]{0:T(128)} %copy-done.1, bf16[4,8,2,128,128]{4,3,2,1,0:T(8,128)(2,1)} %get-tuple-element.9.fin_ref, f32[4,16,128]{2,1,0:T(8,128)} %get-tuple-element.10.tails_ref, ...), custom_call_target="tpu_custom_call" | custom-call | tf_op jit(solution)/shard_map/unpack/pallas_call | solution.py:383
  (4 shorter events, 0.0 us)
Async XLA Ops:
  2.0 81.2 %copy-start.1 = (s32[32]{0:T(128)}, s32[32]{0:T(128)S(1)}, u32[]{:S(2)}) copy-start(s32[32]{0:T(128)S(1)} %fusion.1.slot) | copy-start | bytes 388
  2.1 81.2 %copy-start.2 = (s32[32]{0:T(128)}, s32[32]{0:T(128)S(1)}, u32[]{:S(2)}) copy-start(s32[32]{0:T(128)S(1)} %get-tuple-element.19.owner) | copy-start | bytes 388
  2.3 81.0 %copy-start.3 = (s32[32]{0:T(128)}, s32[32]{0:T(128)S(1)}, u32[]{:S(2)}) copy-start(s32[32]{0:T(128)S(1)} %convert_reduce_fusion.rank) | copy-start | bytes 388
  2.9 0.7 copy-start
